TPU v7x, 128 devices: a whole 4x4x4 slice. The times are simulated.
128 devices in a mesh: gx: 8 (over z, core), gy: 16 (over x, y).
Axes of the slice: x: 4, y: 4, z: 4, core: 2. Of those that a mesh axis runs over, the one named last changes fastest.
Arguments:
- conductivity: float32 [16, 512, 2048], P(None, 'gx', 'gy'), may hold values from 0.1 to 10
- well_rates: float32 [16, 512, 2048], P(None, 'gx', 'gy'), may hold values from -384 to 384
- block_label: int32 [512, 2048], P('gx', 'gy'), may hold values from 0 to 1023, as said below
- owned_pairs: int32 [1024], P(('gx', 'gy')), may hold values from 0 to 1023, each once
Outputs:
- fine_flux: float32 [3, 16, 512, 2048], P(None, None, 'gx', 'gy')
- coarse_flux: float32 [1024], P(('gx', 'gy'))
Inputs may be any that keep to these rules, and one draw needn't show every extreme that they name: `block_label`: label = column * 64 + row, with column = ((x + o) // 32) % 16 for an offset o of 0 to 31 that is fixed for each fine row y, and row = ((y + q) // 32) % 64 for an offset q of 0 to 31 that is fixed for each fine column x. `owned_pairs`: each pair number once; the pairs in one device's shard are owned by that device.
All inputs are finite; a program needn't handle non-finite values.
Results may differ from a plain program's by a relative error of at most 0.0003.
Values sent between devices are 32-bit elements; how exact they have to be, the bound alone decides.
A program may use at most 128 MiB of HBM per device.

v0:
```python
import jax
import jax.numpy as jnp
from jax import lax
from jax.sharding import Mesh
from jax.sharding import PartitionSpec as P

BX = 32
BY = 32
ITERS = 13
GX = ("gx_0", "gx_1")
GY = ("gy_0", "gy_1")
GX_GY = ("gx_0", "gx_1", "gy_0", "gy_1")


REACTION = 0.05
RELAXATION = 0.8


def with_halo(block, sides, width):
    for axis, dim in sides:
        count = lax.axis_size(axis)
        forward = [(i, i + 1) for i in range(count - 1)]
        forward.append((count - 1, 0))
        backward = [(target, source) for source, target in forward]
        low = lax.ppermute(
            lax.slice_in_dim(block, block.shape[dim] - width, None, axis=dim), axis, forward
        )
        high = lax.ppermute(lax.slice_in_dim(block, 0, width, axis=dim), axis, backward)
        block = jnp.concatenate([low, block, high], axis=dim)
    return block


def by_axis(x, axes):
    for axis in axes:
        x = lax.psum(x, axis)
    return x


def harmonic(one_side, other_side):
    total = one_side + other_side
    return 2.0 * one_side * other_side / jnp.where(total > 0, total, 1.0)


def pair_fields(labels_grid, blocks_x, blocks_y):
    column = labels_grid // blocks_y
    row_index = labels_grid % blocks_y
    first_ids = column // 2 * blocks_y + row_index
    second_ids = (
        (column + blocks_x - 1) % blocks_x // 2 * blocks_y + row_index + blocks_x // 2 * blocks_y
    )
    parity_sign = jnp.where(column % 2 == 0, 1.0, -1.0).astype(jnp.float32)
    return (jnp.stack([first_ids, second_ids]), jnp.stack([parity_sign, -parity_sign]))


def shift_up(field):
    return jnp.concatenate([field[:, 1:], jnp.zeros_like(field[:, :1])], axis=1)


def shift_down(field):
    return jnp.concatenate([jnp.zeros_like(field[:, :1]), field[:, :-1]], axis=1)


def shards(conductivity, well_rates, block_label, owned_pairs):
    layers, cells_x, cells_y = conductivity.shape
    blocks_x = cells_x * lax.axis_size(GX) // BX
    blocks_y = cells_y * lax.axis_size(GY) // BY
    pair_count = blocks_x * blocks_y
    stacked = jnp.concatenate([conductivity, block_label.astype(jnp.float32)[None]], axis=0)
    margin = ITERS + 1
    padded = with_halo(stacked, ((GX, 1), (GY, 2)), ITERS + 1)
    cond_pad = padded[:layers]
    label_pad = padded[layers].astype(jnp.int32)
    ids_pad, signs_pad = pair_fields(label_pad, blocks_x, blocks_y)
    same_x = ids_pad[:, :-1, :] == ids_pad[:, 1:, :]
    same_y = ids_pad[:, :, :-1] == ids_pad[:, :, 1:]
    trans_x = jnp.where(
        same_x[:, None], harmonic(cond_pad[:, :-1, :], cond_pad[:, 1:, :])[None], 0.0
    )
    trans_y = jnp.where(
        same_y[:, None], harmonic(cond_pad[:, :, :-1], cond_pad[:, :, 1:])[None], 0.0
    )
    vertical = harmonic(cond_pad[:-1], cond_pad[1:])
    flat_layer = jnp.zeros((1,) + vertical.shape[1:], jnp.float32)
    trans_z = jnp.concatenate([flat_layer, vertical, flat_layer], axis=0)

    def face_terms(offset, count_x, count_y):
        plus_x = trans_x[:, :, offset : offset + count_x, offset : offset + count_y]
        minus_x = trans_x[:, :, offset - 1 : offset - 1 + count_x, offset : offset + count_y]
        plus_y = trans_y[:, :, offset : offset + count_x, offset : offset + count_y]
        minus_y = trans_y[:, :, offset : offset + count_x, offset - 1 : offset - 1 + count_y]
        plus_z = trans_z[1:, offset : offset + count_x, offset : offset + count_y]
        minus_z = trans_z[:-1, offset : offset + count_x, offset : offset + count_y]
        return (plus_x, minus_x, plus_y, minus_y, plus_z, minus_z)

    inner_x = cells_x + 2 * margin - 2
    inner_y = cells_y + 2 * margin - 2
    plus_x, minus_x, plus_y, minus_y, plus_z, minus_z = face_terms(1, inner_x, inner_y)
    diag_full = REACTION + plus_x + minus_x + plus_y + minus_y + plus_z + minus_z
    source_full = jnp.broadcast_to(signs_pad[:, None, 1:-1, 1:-1], diag_full.shape)

    def sweep(padded_field, rim_width):
        offset = margin - rim_width + 1
        count_x = cells_x + 2 * (rim_width - 1)
        count_y = cells_y + 2 * (rim_width - 1)
        face_x, back_x, face_y, back_y, face_up, face_down = face_terms(offset, count_x, count_y)
        centre = padded_field[:, :, 1:-1, 1:-1]
        applied = (
            REACTION * centre
            + face_x * (centre - padded_field[:, :, 2:, 1:-1])
            + back_x * (centre - padded_field[:, :, :-2, 1:-1])
            + face_y * (centre - padded_field[:, :, 1:-1, 2:])
            + back_y * (centre - padded_field[:, :, 1:-1, :-2])
            + face_up * (centre - shift_up(centre))
            + face_down * (centre - shift_down(centre))
        )
        return centre + RELAXATION * (source_full - applied) / diag_full

    start_field = RELAXATION * source_full / diag_full

    def wide_step(step_index, field):
        bordered = jnp.pad(field, ((0, 0), (0, 0), (1, 1), (1, 1)))
        return sweep(bordered, margin)

    field = lax.fori_loop(0, ITERS - 1, wide_step, start_field)
    final_pad = field[:, :, margin - 2 : margin + cells_x, margin - 2 : margin + cells_y]
    pressure = final_pad[:, :, 1:-1, 1:-1]
    next_x = final_pad[:, :, 2:, 1:-1]
    next_y = final_pad[:, :, 1:-1, 2:]
    face_x, back_x, face_y, back_y, face_up, face_down = face_terms(margin, cells_x, cells_y)
    diff_x = pressure - next_x
    diff_y = pressure - next_y
    diff_z = pressure - shift_up(pressure)
    flux_x = face_x * diff_x
    flux_y = face_y * diff_y
    flux_z = face_up * diff_z
    energy = jnp.sum(
        flux_x * diff_x + flux_y * diff_y + flux_z * diff_z + REACTION * pressure * pressure, axis=1
    )
    load_cell = jnp.sum(well_rates[None] * pressure, axis=1)
    ids_own = ids_pad[:, margin : margin + cells_x, margin : margin + cells_y]
    flat_ids = ids_own.reshape(-1)
    energy_sum = jax.ops.segment_sum(energy.reshape(-1), flat_ids, num_segments=pair_count)
    load_sum = jax.ops.segment_sum(load_cell.reshape(-1), flat_ids, num_segments=pair_count)
    partial_value = jnp.stack([energy_sum, load_sum])
    totals = by_axis(partial_value, GX_GY)
    all_rates = totals[1] / totals[0]
    coarse = jnp.take(all_rates, owned_pairs)
    weight = jnp.take(all_rates, ids_own)[:, None]
    fine_flux_out = jnp.stack(
        [
            jnp.sum(weight * flux_x, axis=0),
            jnp.sum(weight * flux_y, axis=0),
            jnp.sum(weight * flux_z, axis=0),
        ]
    )
    return (fine_flux_out, coarse)


def solution(mesh):
    finer = Mesh(mesh.devices.reshape(4, 2, 4, 4), ("gx_0", "gx_1", "gy_0", "gy_1"))
    in_specs = (P(None, GX, GY), P(None, GX, GY), P(GX, GY), P(GX_GY))
    out_specs = (P(None, None, GX, GY), P(GX_GY))
    return jax.shard_map(
        shards, mesh=finer, in_specs=in_specs, out_specs=out_specs, check_vma=False
    )
```

profile of v0, /device:TPU:1, one launch (start us, length us, event | category | flops | bytes accessed | tf_op | source)
XLA Modules:
  0.0 620.6 jit_solution(6867308519037712772)
XLA Ops:
  12.0 5.0 collective-permute-start.3
  17.0 8.0 %collective-permute-done.2 = f32[17,92,14]{1,2,0:T(8,128)S(1)} collective-permute-done((f32[17,92,14]{1,2,0:T(8,128)S(1)}, f32[17,92,14]{1,2,0:T(8,128)S(1)}, u32[]{:S(2)}, u32[]{:S(2)}) %collective-permute-start.2) | collective-permute-done | bytes 87616 | tf_op jit(solution)/shard_map/ppermute | solution.py:25
  32.7 4.6 broadcast_divide_fusion
  37.3 249.1 %while.13 = (s32[]{:T(128)}, f32[2,16,90,154]{3,2,1,0:T(8,128)}, f32[2,16,91,156]{3,2,1,0:T(8,128)}, f32[2,16,92,155]{3,2,1,0:T(8,128)}, f32[17,92,156]{2,1,0:T(...) while((s32[]{:T(128)}, f32[2,16,90,154]{3,2,1,0:T(8,128)}, ...), condition=%wide.region_1.2_spmd.clone, body=%wide.region_0.1_spmd.clone.sunk | while | flops 10200962 | bytes 35282896 | solution.py:124
  42.2 3.6 fusion.50
  45.8 12.3 %divide_add_fusion.2 = f32[2,16,90,154]{3,2,1,0:T(8,128)} fusion(f32[2,16,90,154]{3,2,1,0:T(8,128)S(1)} %copy.32, f32[2,16,90,154]{3,2,1,0:T(8,128)} %get-tuple-element.228, f32[2,15,90,154]{3,2,1,0:T(8,128)} %get-tuple-element.203, f32[2,15,90,154]{3,2,1,0:T(8,128)} %get-tuple-element.204, f32[2,16,92,155]{3,2,1,0:T(8,128)} %get-tuple-element.226, ...), kind=kLoop, calls=%fused_computation.5.clone.1 | loop fusion | flops 10200960 | bytes 17629920 | tf_op jit(solution)/shard_map/while/body/eval_jaxpr/add | solution.py:116
  63.0 3.6 fusion.50
  66.6 12.3 %divide_add_fusion.2 = f32[2,16,90,154]{3,2,1,0:T(8,128)} fusion(f32[2,16,90,154]{3,2,1,0:T(8,128)S(1)} %copy.32, f32[2,16,90,154]{3,2,1,0:T(8,128)} %get-tuple-element.228, f32[2,15,90,154]{3,2,1,0:T(8,128)} %get-tuple-element.203, f32[2,15,90,154]{3,2,1,0:T(8,128)} %get-tuple-element.204, f32[2,16,92,155]{3,2,1,0:T(8,128)} %get-tuple-element.226, ...), kind=kLoop, calls=%fused_computation.5.clone.1 | loop fusion | flops 10200960 | bytes 17629920 | tf_op jit(solution)/shard_map/while/body/eval_jaxpr/add | solution.py:116
  83.7 3.6 fusion.50
  87.3 12.3 %divide_add_fusion.2 = f32[2,16,90,154]{3,2,1,0:T(8,128)} fusion(f32[2,16,90,154]{3,2,1,0:T(8,128)S(1)} %copy.32, f32[2,16,90,154]{3,2,1,0:T(8,128)} %get-tuple-element.228, f32[2,15,90,154]{3,2,1,0:T(8,128)} %get-tuple-element.203, f32[2,15,90,154]{3,2,1,0:T(8,128)} %get-tuple-element.204, f32[2,16,92,155]{3,2,1,0:T(8,128)} %get-tuple-element.226, ...), kind=kLoop, calls=%fused_computation.5.clone.1 | loop fusion | flops 10200960 | bytes 17629920 | tf_op jit(solution)/shard_map/while/body/eval_jaxpr/add | solution.py:116
  104.5 3.6 fusion.50
  108.1 12.3 %divide_add_fusion.2 = f32[2,16,90,154]{3,2,1,0:T(8,128)} fusion(f32[2,16,90,154]{3,2,1,0:T(8,128)S(1)} %copy.32, f32[2,16,90,154]{3,2,1,0:T(8,128)} %get-tuple-element.228, f32[2,15,90,154]{3,2,1,0:T(8,128)} %get-tuple-element.203, f32[2,15,90,154]{3,2,1,0:T(8,128)} %get-tuple-element.204, f32[2,16,92,155]{3,2,1,0:T(8,128)} %get-tuple-element.226, ...), kind=kLoop, calls=%fused_computation.5.clone.1 | loop fusion | flops 10200960 | bytes 17629920 | tf_op jit(solution)/shard_map/while/body/eval_jaxpr/add | solution.py:116
  125.3 3.6 fusion.50
  128.8 12.3 %divide_add_fusion.2 = f32[2,16,90,154]{3,2,1,0:T(8,128)} fusion(f32[2,16,90,154]{3,2,1,0:T(8,128)S(1)} %copy.32, f32[2,16,90,154]{3,2,1,0:T(8,128)} %get-tuple-element.228, f32[2,15,90,154]{3,2,1,0:T(8,128)} %get-tuple-element.203, f32[2,15,90,154]{3,2,1,0:T(8,128)} %get-tuple-element.204, f32[2,16,92,155]{3,2,1,0:T(8,128)} %get-tuple-element.226, ...), kind=kLoop, calls=%fused_computation.5.clone.1 | loop fusion | flops 10200960 | bytes 17629920 | tf_op jit(solution)/shard_map/while/body/eval_jaxpr/add | solution.py:116
  149.6 12.3 %divide_add_fusion.2 = f32[2,16,90,154]{3,2,1,0:T(8,128)} fusion(f32[2,16,90,154]{3,2,1,0:T(8,128)S(1)} %copy.32, f32[2,16,90,154]{3,2,1,0:T(8,128)} %get-tuple-element.228, f32[2,15,90,154]{3,2,1,0:T(8,128)} %get-tuple-element.203, f32[2,15,90,154]{3,2,1,0:T(8,128)} %get-tuple-element.204, f32[2,16,92,155]{3,2,1,0:T(8,128)} %get-tuple-element.226, ...), kind=kLoop, calls=%fused_computation.5.clone.1 | loop fusion | flops 10200960 | bytes 17629920 | tf_op jit(solution)/shard_map/while/body/eval_jaxpr/add | solution.py:116
  166.8 3.6 fusion.50
  170.3 12.3 %divide_add_fusion.2 = f32[2,16,90,154]{3,2,1,0:T(8,128)} fusion(f32[2,16,90,154]{3,2,1,0:T(8,128)S(1)} %copy.32, f32[2,16,90,154]{3,2,1,0:T(8,128)} %get-tuple-element.228, f32[2,15,90,154]{3,2,1,0:T(8,128)} %get-tuple-element.203, f32[2,15,90,154]{3,2,1,0:T(8,128)} %get-tuple-element.204, f32[2,16,92,155]{3,2,1,0:T(8,128)} %get-tuple-element.226, ...), kind=kLoop, calls=%fused_computation.5.clone.1 | loop fusion | flops 10200960 | bytes 17629920 | tf_op jit(solution)/shard_map/while/body/eval_jaxpr/add | solution.py:116
  191.1 12.3 %divide_add_fusion.2 = f32[2,16,90,154]{3,2,1,0:T(8,128)} fusion(f32[2,16,90,154]{3,2,1,0:T(8,128)S(1)} %copy.32, f32[2,16,90,154]{3,2,1,0:T(8,128)} %get-tuple-element.228, f32[2,15,90,154]{3,2,1,0:T(8,128)} %get-tuple-element.203, f32[2,15,90,154]{3,2,1,0:T(8,128)} %get-tuple-element.204, f32[2,16,92,155]{3,2,1,0:T(8,128)} %get-tuple-element.226, ...), kind=kLoop, calls=%fused_computation.5.clone.1 | loop fusion | flops 10200960 | bytes 17629920 | tf_op jit(solution)/shard_map/while/body/eval_jaxpr/add | solution.py:116
  208.3 3.6 fusion.50
  211.8 12.3 %divide_add_fusion.2 = f32[2,16,90,154]{3,2,1,0:T(8,128)} fusion(f32[2,16,90,154]{3,2,1,0:T(8,128)S(1)} %copy.32, f32[2,16,90,154]{3,2,1,0:T(8,128)} %get-tuple-element.228, f32[2,15,90,154]{3,2,1,0:T(8,128)} %get-tuple-element.203, f32[2,15,90,154]{3,2,1,0:T(8,128)} %get-tuple-element.204, f32[2,16,92,155]{3,2,1,0:T(8,128)} %get-tuple-element.226, ...), kind=kLoop, calls=%fused_computation.5.clone.1 | loop fusion | flops 10200960 | bytes 17629920 | tf_op jit(solution)/shard_map/while/body/eval_jaxpr/add | solution.py:116
  232.6 12.3 %divide_add_fusion.2 = f32[2,16,90,154]{3,2,1,0:T(8,128)} fusion(f32[2,16,90,154]{3,2,1,0:T(8,128)S(1)} %copy.32, f32[2,16,90,154]{3,2,1,0:T(8,128)} %get-tuple-element.228, f32[2,15,90,154]{3,2,1,0:T(8,128)} %get-tuple-element.203, f32[2,15,90,154]{3,2,1,0:T(8,128)} %get-tuple-element.204, f32[2,16,92,155]{3,2,1,0:T(8,128)} %get-tuple-element.226, ...), kind=kLoop, calls=%fused_computation.5.clone.1 | loop fusion | flops 10200960 | bytes 17629920 | tf_op jit(solution)/shard_map/while/body/eval_jaxpr/add | solution.py:116
  253.4 12.3 %divide_add_fusion.2 = f32[2,16,90,154]{3,2,1,0:T(8,128)} fusion(f32[2,16,90,154]{3,2,1,0:T(8,128)S(1)} %copy.32, f32[2,16,90,154]{3,2,1,0:T(8,128)} %get-tuple-element.228, f32[2,15,90,154]{3,2,1,0:T(8,128)} %get-tuple-element.203, f32[2,15,90,154]{3,2,1,0:T(8,128)} %get-tuple-element.204, f32[2,16,92,155]{3,2,1,0:T(8,128)} %get-tuple-element.226, ...), kind=kLoop, calls=%fused_computation.5.clone.1 | loop fusion | flops 10200960 | bytes 17629920 | tf_op jit(solution)/shard_map/while/body/eval_jaxpr/add | solution.py:116
  274.1 12.3 %divide_add_fusion.2 = f32[2,16,90,154]{3,2,1,0:T(8,128)} fusion(f32[2,16,90,154]{3,2,1,0:T(8,128)S(1)} %copy.32, f32[2,16,90,154]{3,2,1,0:T(8,128)} %get-tuple-element.228, f32[2,15,90,154]{3,2,1,0:T(8,128)} %get-tuple-element.203, f32[2,15,90,154]{3,2,1,0:T(8,128)} %get-tuple-element.204, f32[2,16,92,155]{3,2,1,0:T(8,128)} %get-tuple-element.226, ...), kind=kLoop, calls=%fused_computation.5.clone.1 | loop fusion | flops 10200960 | bytes 17629920 | tf_op jit(solution)/shard_map/while/body/eval_jaxpr/add | solution.py:116
  288.3 6.5 %fusion.15 = (f32[2,64,128]{2,1,0:T(8,128)S(1)}, f32[2,64,128]{2,1,0:T(8,128)S(1)}) fusion(f32[2,15,64,128]{3,2,1,0:T(8,128)S(1)} %slice.213, f32[2,16,90,154]{3,2,1,0:T(8,128)} %get-tuple-element.91, f32[16,64,128]{2,1,0:T(8,128)} %pad_slice_fusion.3, f32[2,16,91,156]{3,2,1,0:T(8,128)} %get-tuple-element.232, f32[2,16,92,155]{3,2,1,0:T(8,128)} %get-tuple-element.231, ...), kind=kLoop, calls=%fused_computation.40 | loop fusion | flops 4423680 | bytes 7405568 | tf_op jit(solution)/shard_map/reduce_sum | solution.py:136
  294.8 113.4 %scatter_custom_fusion = f32[1024]{0:T(1024)S(1)} fusion(s32[16384]{0:T(1024)S(1)} %bitcast.18, f32[16384]{0:T(1024)S(1)} %bitcast.23, f32[]{:T(128)} %constant.142.clone.1), kind=kCustom, calls=%fused_computation.115 | custom fusion | flops 16384 | bytes 4100 | tf_op jit(solution)/shard_map/scatter-add | solution.py:142
  408.3 113.4 %scatter_custom_fusion.1 = f32[1024]{0:T(1024)S(1)} fusion(s32[16384]{0:T(1024)S(1)} %bitcast.19, f32[16384]{0:T(1024)S(1)} %bitcast.22, f32[]{:T(128)} %constant.142.clone.1), kind=kCustom, calls=%fused_computation.113 | custom fusion | flops 16384 | bytes 4100 | tf_op jit(solution)/shard_map/scatter-add | solution.py:143
  521.7 9.7 %psum.28 = f32[2,1024]{1,0:T(2,128)S(1)} all-reduce(f32[2,1024]{1,0:T(2,128)S(1)} %pad_maximum_fusion.7), channel_id=1, replica_groups=mesh['gx_0'=4,'gx_1'=2,'gy_0'=4,'gy_1'=4] {'gx_0'}, use_global_device_ids=true, to_apply=%region_6.7 | all-reduce | flops 2048 | bytes 16384 | tf_op jit(solution)/shard_map/psum | solution.py:35
  531.4 4.8 psum.29
  536.2 6.1 psum.30
  542.3 6.1 psum.31
  549.1 65.3 %gather_fusion = f32[16384]{0:T(1024)S(1)} fusion(f32[1024]{0:T(1024)S(1)} %bitcast.14, s32[16384]{0:T(1024)S(1)} %broadcast_clamp_fusion), kind=kCustom, calls=%fused_computation | custom fusion | bytes 196608 | tf_op jit(solution)/shard_map/jit(_take)/gather | solution.py:148
  614.4 4.4 multiply_reduce_fusion.1
  (105 shorter events, 100.3 us)
Async XLA Ops:
  2.4 5.1 collective-permute-start
  5.4 4.5 collective-permute-start.1
  11.0 14.7 %copy-start.5 = (f32[16,64,128]{2,1,0:T(8,128)S(1)}, f32[16,64,128]{2,1,0:T(8,128)}, u32[]{:S(2)}) copy-start(f32[16,64,128]{2,1,0:T(8,128)} %param.6) | copy-start | bytes 1572868
  12.0 13.4 %collective-permute-start.3 = (f32[17,92,14]{1,2,0:T(8,128)S(1)}, f32[17,92,14]{1,2,0:T(8,128)S(1)}, u32[]{:S(2)}, u32[]{:S(2)}) collective-permute-start(f32[17,92,14]{1,2,0:T(8,128)S(1)} %copy.20), channel_id=1, source_target_pairs={{1,0},{2,1},{3,2},{4,3},{5,4},{6,5},{7,6},{8,7},{9,8},{10,9},{11,1... | collective-permute-start | bytes 262760 | tf_op jit(solution)/shard_map/ppermute | solution.py:28
  17.0 8.1 %collective-permute-start.2 = (f32[17,92,14]{1,2,0:T(8,128)S(1)}, f32[17,92,14]{1,2,0:T(8,128)S(1)}, u32[]{:S(2)}, u32[]{:S(2)}) collective-permute-start(f32[17,92,14]{1,2,0:T(8,128)S(1)} %copy.19), channel_id=1, source_target_pairs={{0,1},{1,2},{2,3},{3,4},{4,5},{5,6},{6,7},{7,8},{8,9},{9,10},{10,1... | collective-permute-start | bytes 262760 | tf_op jit(solution)/shard_map/ppermute | solution.py:25
  32.3 4.9 copy-start
  32.7 4.6 copy-start.1
  37.3 2.4 copy-start.3
  58.1 2.4 copy-start.3
  78.8 2.4 copy-start.3
  99.6 2.4 copy-start.3
  120.3 2.4 copy-start.3
  141.1 2.4 copy-start.3
  161.8 2.4 copy-start.3
  182.6 2.4 copy-start.3
  203.3 2.4 copy-start.3
  224.1 2.4 copy-start.3
  244.9 2.4 copy-start.3
  265.6 2.4 copy-start.3
  288.3 6.5 %copy-start.4 = (f32[2,15,64,128]{3,2,1,0:T(8,128)}, f32[2,15,64,128]{3,2,1,0:T(8,128)S(1)}, u32[]{:S(2)}) copy-start(f32[2,15,64,128]{3,2,1,0:T(8,128)S(1)} %slice.213) | copy-start | bytes 2949124
  549.1 65.3 %copy-start.2 = (f32[2,16,90,154]{3,2,1,0:T(8,128)S(1)}, f32[2,16,90,154]{3,2,1,0:T(8,128)}, u32[]{:S(2)}) copy-start(f32[2,16,90,154]{3,2,1,0:T(8,128)} %get-tuple-element.91) | copy-start | bytes 5322244
  614.4 4.5 copy-start.6
where the time goes:
time: 624 us; the launch traced here: 621 us
  other arithmetic  400 us (64%)
  local copies, waits for them, and re-layouts  173 us (28%)
  blocking collectives  26.7 us (4%)
  waiting for transfers between devices  11.9 us (2%)
  starting transfers between devices  8.02 us (1%)
    add x12, other arithmetic, sweep(): return centre + RELAXATION * (source_full - applied) / diag_full  147 us
    scatter-add x1, other arithmetic, shards(): jax.ops.segment_sum(energy.reshape(-1), flat_ids, num_segments=pair_count)  113 us
    scatter-add x1, other arithmetic, shards(): jax.ops.segment_sum(load_cell.reshape(-1), flat_ids, num_segments=pair_co...  113 us
    gather x1, local copies, waits for them, and re-layouts, shards(): weight = jnp.take(all_rates, ids_own)[:, None]  65.3 us
    slice x13, local copies, waits for them, and re-layouts, shift_up(): return jnp.concatenate([field[:, 1:], jnp.zeros_like(field[:, :1])], axis=1)  44.8 us
    slice x14, local copies, waits for them, and re-layouts, face_terms(): plus_z = trans_z[1:, offset:offset + count_x, offset:offset + count_y]  32.3 us
    while x36, local copies, waits for them, and re-layouts  28.6 us
    psum x4, blocking collectives, by_axis(): x = lax.psum(x, axis)  26.7 us
  transfers between devices with their start and end apart: 4, of which 3 were waited for; matrix products, arithmetic and copies ran while one was open for 0% of the time, Pallas kernels for 0%

commit v1 on v0

v1 whole, which is shorter than its diff:
```python
import functools

import jax
import jax.numpy as jnp
from jax import lax
from jax.experimental import pallas as pl
from jax.experimental.pallas import tpu as pltpu
from jax.sharding import PartitionSpec as P

ITERS = 13
REACTION = 0.05
RELAXATION = 0.8
NZ = 16
CX = 64
CY = 128
HALO = 16
EXT = CX + 2 * HALO
PAD = 8
ROWS = EXT + 2 * PAD
NBINS = 10
MESH = pl.DeviceIdType.MESH
f32 = jnp.float32


def lane_iota():
    return lax.broadcasted_iota(jnp.int32, (8, 128), 1)


def roll(value, shift):
    return pltpu.roll(value, shift % 128, 1)


class Seams:
    def __init__(self):
        lane = lane_iota()
        self.group = ((lane + 16) & 127) >> 5
        inner = lane & 31
        self.first = [lane == 32 * g for g in range(4)]
        self.last = [lane == (32 * g - 1) % 128 for g in range(4)]
        self.any_first = inner == 0
        self.any_last = inner == 31
        self.right_half = inner < 16

    def compose(self, own):
        return jnp.where(
            self.group < 2,
            jnp.where(self.group < 1, own[0], own[1]),
            jnp.where(self.group < 3, own[2], own[3]),
        )

    def right(self, own, strip, mixed):
        out = [roll(jnp.where(self.first[g], strip, own[g]), -1) for g in range(4)]
        return out, roll(jnp.where(self.any_first, mixed, strip), -1)

    def left(self, own, strip, mixed):
        out = [roll(jnp.where(self.last[g], strip, own[g]), 1) for g in range(4)]
        return out, roll(jnp.where(self.any_last, mixed, strip), 1)


def both_sides(seams, own20, left=True):
    right, lefts = [None] * 20, [None] * 20
    for k in range(4):
        own = [own20[4 * g + k] for g in range(4)]
        strip = own20[16 + k]
        mixed = seams.compose(own)
        out, edge = seams.right(own, strip, mixed)
        for g in range(4):
            right[4 * g + k] = out[g]
        right[16 + k] = edge
        if left:
            out, edge = seams.left(own, strip, mixed)
            for g in range(4):
                lefts[4 * g + k] = out[g]
            lefts[16 + k] = edge
    return right, lefts


def plane_of(i):
    return i // 4 if i < 16 else 4


def layer_above(values, i):
    if i % 4 != 3:
        return values[i + 1]
    return roll(values[i + 1 if i < NZ - 1 else 16 if i == 19 else 0], -32)


def layer_below(values, i):
    if i % 4 != 0:
        return values[i - 1]
    return roll(values[19 if i == 16 else i - 1], 32)


def harmonic(one, other):
    return 2.0 * one * other / (one + other)


def pair_ids(label, row_bits, columns):
    column = label >> row_bits
    row = label & ((1 << row_bits) - 1)
    first = ((column >> 1) << row_bits) + row
    second = ((((column + columns - 1) & (columns - 1)) >> 1) << row_bits) + row + ((columns // 2) << row_bits)
    sign = jnp.where((column & 1) == 0, 1.0, -1.0).astype(f32)
    return first, second, sign


def kernel(gx, gy, cond, well, label, owned, fine, coarse, ce, le, wl, send_l, send_r, from_l, from_r,
           c, ids, tx, ty, tyb, hz, hzb, w, s, p, flux, sums, part, gathered, staged,
           local_sem, out_sem, halo_send, halo_recv, row_send, row_recv, col_send, col_recv):
    m, n = lax.axis_index("gx"), lax.axis_index("gy")
    row_bits = (4 * gy).bit_length() - 1
    columns = 2 * gx

    def at(dm, dn):
        return (lax.rem(m + dm + gx, gx), lax.rem(n + dn + gy, gy))

    partners = [at(d, 0) for d in range(1, gx)] + [at(0, d) for d in range(1, gy)]
    partners += [at(a, b) for a in (-1, 1) for b in (-1, 1)]
    barrier = pltpu.get_barrier_semaphore()
    for partner in partners:
        pl.semaphore_signal(barrier, inc=1, device_id=partner, device_id_type=MESH)

    own_rows = pl.ds(HALO, CX)
    loads = [
        pltpu.make_async_copy(cond, ce.at[:, own_rows], local_sem.at[0]),
        pltpu.make_async_copy(label, le.at[own_rows], local_sem.at[1]),
        pltpu.make_async_copy(well, wl, local_sem.at[2]),
    ]
    for load in loads:
        load.start()

    for f in range(2):
        tx[f, :, :PAD, :] = jnp.zeros((20, PAD, 128), f32)
        for slot in range(2):
            p[slot, f, :, :PAD, :] = jnp.zeros((20, PAD, 128), f32)
            p[slot, f, :, ROWS - PAD :, :] = jnp.zeros((20, PAD, 128), f32)
        for plane in range(5):
            ids[f, plane, ROWS - PAD :, :] = jnp.zeros((PAD, 128), jnp.int32)
    c[:, ROWS - PAD :, :] = jnp.ones((20, PAD, 128), f32)

    loads[0].wait()
    loads[1].wait()

    def pack(xb, carry):
        seams = Seams()
        rows = pl.ds(pl.multiple_of(HALO + 8 * xb, 8), 8)
        out = pl.ds(pl.multiple_of(8 * xb, 8), 8)
        mixed = [
            seams.compose([roll(ce[4 * g + k, rows, :], 32 * g) for g in range(4)]) for k in range(4)
        ]
        for h in range(2):
            even, odd = mixed[2 * h], roll(mixed[2 * h + 1], 16)
            send_l[h, out, :] = jnp.where(seams.right_half, even, odd)
            send_r[h, out, :] = jnp.where(seams.right_half, odd, even)
        tags = seams.compose([roll(le[rows, :], 32 * g) for g in range(4)]).astype(f32)
        send_l[2, out, :] = tags
        send_r[2, out, :] = tags
        return carry

    lax.fori_loop(0, CX // 8, pack, 0)
    pl.semaphore_wait(barrier, len(partners))

    low, high = pl.ds(0, HALO), pl.ds(CX - HALO, HALO)
    below, above = pl.ds(0, HALO), pl.ds(HALO + CX, HALO)
    moves = [
        (cond.at[:, low], ce.at[:, above], at(-1, 0)),
        (cond.at[:, high], ce.at[:, below], at(1, 0)),
        (label.at[low], le.at[above], at(-1, 0)),
        (label.at[high], le.at[below], at(1, 0)),
        (send_l, from_r.at[:, own_rows], at(0, -1)),
        (send_r, from_l.at[:, own_rows], at(0, 1)),
        (send_l.at[:, low], from_r.at[:, above], at(-1, -1)),
        (send_l.at[:, high], from_r.at[:, below], at(1, -1)),
        (send_r.at[:, low], from_l.at[:, above], at(-1, 1)),
        (send_r.at[:, high], from_l.at[:, below], at(1, 1)),
    ]
    halos = [
        pltpu.make_async_remote_copy(src, dst, halo_send.at[i], halo_recv.at[i], device_id=to, device_id_type=MESH)
        for i, (src, dst, to) in enumerate(moves)
    ]
    for halo in halos:
        halo.start()
    for halo in halos:
        halo.wait()

    def assemble(xb, carry):
        seams = Seams()
        rows = pl.ds(pl.multiple_of(8 * xb, 8), 8)
        out = pl.ds(pl.multiple_of(PAD + 8 * xb, 8), 8)
        for z in range(NZ):
            c[z, out, :] = roll(ce[z, rows, :], 32 * (z // 4))
        for h in range(2):
            right, left = from_r[h, rows, :], from_l[h, rows, :]
            c[16 + 2 * h, out, :] = jnp.where(seams.right_half, right, left)
            c[17 + 2 * h, out, :] = jnp.where(seams.right_half, roll(right, -16), roll(left, -16))
        tags = jnp.where(seams.right_half, from_r[2, rows, :], from_l[2, rows, :]).astype(jnp.int32)
        labels = [roll(le[rows, :], 32 * g) for g in range(4)] + [tags]
        for plane in range(5):
            first, second, sign = pair_ids(labels[plane], row_bits, columns)
            ids[0, plane, out, :] = first
            ids[1, plane, out, :] = second
            s[0, plane, out, :] = sign
            s[1, plane, out, :] = -sign
        return carry

    lax.fori_loop(0, EXT // 8, assemble, 0)

    def faces(xb, carry):
        seams = Seams()
        a = PAD + 8 * xb
        here, ahead = pl.ds(pl.multiple_of(a, 8), 8), pl.ds(a + 1, 8)
        cs = [c[i, here, :] for i in range(20)]
        right, _ = both_sides(seams, cs, left=False)
        hx = [harmonic(cs[i], c[i, ahead, :]) for i in range(20)]
        hy = [harmonic(cs[i], right[i]) for i in range(20)]
        for i in range(20):
            face = jnp.zeros((8, 128), f32)
            if i != NZ - 1:
                face = harmonic(cs[i], layer_above(cs, i))
            if i == 19:
                face = jnp.where(seams.group == 3, 0.0, face)
            hz[i, here, :] = face
            if i % 4 == 3 and i != NZ - 1:
                hzb[i // 4, here, :] = roll(face, 32)
        for f in range(2):
            pid = [ids[f, plane, here, :] for plane in range(5)]
            same_x = [pid[plane] == ids[f, plane, ahead, :] for plane in range(5)]
            out, edge = seams.right(pid[:4], pid[4], seams.compose(pid[:4]))
            same_y = [one == other for one, other in zip(pid, out + [edge])]
            tys = [jnp.where(same_y[plane_of(i)], hy[i], 0.0) for i in range(20)]
            _, back = both_sides(seams, tys)
            for i in range(20):
                tx[f, i, here, :] = jnp.where(same_x[plane_of(i)], hx[i], 0.0)
                ty[f, i, here, :] = tys[i]
                tyb[f, i, here, :] = back[i]
        return carry

    lax.fori_loop(0, EXT // 8, faces, 0)

    def face_below(i, here):
        if i % 4 != 0:
            return hz[i - 1, here, :]
        return hzb[4 if i == 16 else i // 4 - 1, here, :]

    def weights(xb, carry):
        a = PAD + 8 * xb
        here, behind = pl.ds(pl.multiple_of(a, 8), 8), pl.ds(a - 1, 8)
        for f in range(2):
            for i in range(20):
                total = tx[f, i, here, :] + tx[f, i, behind, :] + ty[f, i, here, :] + tyb[f, i, here, :]
                total += hz[i, here, :] + REACTION
                if i != 0:
                    total += face_below(i, here)
                scale = RELAXATION / total
                w[f, i, here, :] = scale
                p[0, f, i, here, :] = s[f, plane_of(i), here, :] * scale
        return carry

    lax.fori_loop(0, EXT // 8, weights, 0)

    def sweep(src, first, last):
        def step(it, carry):
            f, xb = it & 1, first + (it >> 1)
            seams = Seams()
            a = PAD + 8 * xb
            here, ahead, behind = pl.ds(pl.multiple_of(a, 8), 8), pl.ds(a + 1, 8), pl.ds(a - 1, 8)
            ps = [p[src, f, i, here, :] for i in range(20)]
            right, left = both_sides(seams, ps)
            for i in range(20):
                total = s[f, plane_of(i), here, :]
                total += tx[f, i, here, :] * p[src, f, i, ahead, :]
                total += tx[f, i, behind, :] * p[src, f, i, behind, :]
                total += ty[f, i, here, :] * right[i]
                total += tyb[f, i, here, :] * left[i]
                if i != NZ - 1:
                    total += hz[i, here, :] * layer_above(ps, i)
                if i != 0:
                    total += face_below(i, here) * layer_below(ps, i)
                p[1 - src, f, i, here, :] = (1.0 - RELAXATION) * ps[i] + w[f, i, here, :] * total
            return carry

        lax.fori_loop(0, 2 * (last - first), step, 0)

    for k in range(2, ITERS + 1):
        first = (HALO - (ITERS - k)) // 8
        last = (HALO + CX + (ITERS - k)) // 8 + 1
        sweep(k % 2, first, last)
    done = (ITERS + 1) % 2

    loads[2].wait()

    def fluxes(xb, carry):
        seams = Seams()
        a = PAD + HALO + 8 * xb
        here, ahead = pl.ds(pl.multiple_of(a, 8), 8), pl.ds(a + 1, 8)
        own = pl.ds(pl.multiple_of(8 * xb, 8), 8)
        wells = [roll(wl[z, own, :], 32 * (z // 4)) for z in range(NZ)]
        for f in range(2):
            ps = [p[done, f, i, here, :] for i in range(20)]
            right, _ = both_sides(seams, ps, left=False)
            energy, load = jnp.zeros((8, 128), f32), jnp.zeros((8, 128), f32)
            for g in range(4):
                quarter_energy, quarter_load = None, None
                for z in range(4 * g, 4 * g + 4):
                    dx = ps[z] - p[done, f, z, ahead, :]
                    dy = ps[z] - right[z]
                    vx = tx[f, z, here, :] * dx
                    vy = ty[f, z, here, :] * dy
                    cell = vx * dx + vy * dy + REACTION * ps[z] * ps[z]
                    flux[f, 0, z, own, :] = vx
                    flux[f, 1, z, own, :] = vy
                    if z != NZ - 1:
                        dz = ps[z] - layer_above(ps, z)
                        vz = hz[z, here, :] * dz
                        cell += vz * dz
                    else:
                        vz = jnp.zeros((8, 128), f32)
                    flux[f, 2, z, own, :] = vz
                    rated = wells[z] * ps[z]
                    quarter_energy = cell if quarter_energy is None else quarter_energy + cell
                    quarter_load = rated if quarter_load is None else quarter_load + rated
                energy += roll(quarter_energy, -32 * g)
                load += roll(quarter_load, -32 * g)
            sums[f, 0, own, :] = energy
            sums[f, 1, own, :] = load
        return carry

    lax.fori_loop(0, CX // 8, fluxes, 0)

    def bins_of(xb):
        tags = le[HALO + 8 * xb : HALO + 8 * xb + 8, :]
        column = ((tags >> row_bits) - 2 * m) & (columns - 1)
        row = ((tags & ((1 << row_bits) - 1)) - 4 * n) & ((1 << row_bits) - 1)
        return [jnp.where(column >= edge, 5, 0) + row for edge in (2, 1)]

    totals = [[[jnp.zeros((8, 128), f32) for _ in range(NBINS)] for _ in range(2)] for _ in range(2)]
    for xb in range(CX // 8):
        bins = bins_of(xb)
        for f in range(2):
            cells = [sums[f, q, 8 * xb : 8 * xb + 8, :] for q in range(2)]
            for b in range(NBINS):
                hit = bins[f] == b
                for q in range(2):
                    totals[q][f][b] += jnp.where(hit, cells[q], 0.0)
    line = jnp.zeros((1, 128), f32)
    lane_row = lax.broadcasted_iota(jnp.int32, (1, 128), 1)
    for q in range(2):
        for f in range(2):
            for b in range(NBINS):
                value = jnp.sum(totals[q][f][b], axis=0, keepdims=True)
                value = jnp.sum(value, axis=1, keepdims=True)
                line += jnp.where(lane_row == 20 * q + 10 * f + b, value, 0.0)
    part[0] = line
    mine = n * gx + m
    gathered[pl.ds(mine, 1)] = line[None]

    to_row = [
        pltpu.make_async_remote_copy(
            part, gathered.at[pl.ds(mine, 1)], row_send.at[d], row_recv.at[d], device_id=at(d, 0), device_id_type=MESH
        )
        for d in range(1, gx)
    ]
    for copy in to_row:
        copy.start()
    for copy in to_row:
        copy.wait()
    block = pl.ds(n * gx, gx)
    order = sorted(range(1, gy), key=lambda d: min(d, gy - d))
    to_column = {
        d: pltpu.make_async_remote_copy(
            gathered.at[block], gathered.at[block], col_send.at[d], col_recv.at[d], device_id=at(0, d), device_id_type=MESH
        )
        for d in order
    }
    for d in order:
        to_column[d].start()

    lane_full = lax.broadcasted_iota(jnp.int32, (gx, 128), 1)
    row_full = lax.broadcasted_iota(jnp.int32, (gx, 128), 0)
    entry = lane_full % 20
    family = entry // 10
    column_bin = (entry // 5) & 1
    row_bin = entry % 5

    def rows_of(at_n):
        return jnp.concatenate([gathered[at_n * gx + i] for i in range(gx)], axis=0)

    def across_gx(value):
        before = pltpu.roll(pltpu.roll(value, 1, 0), 128 - 5, 1)
        after = pltpu.roll(pltpu.roll(value, gx - 1, 0), 5, 1)
        return value + jnp.where(family == 0, before, after)

    def rates_of(value, previous):
        whole = value + jnp.where(row_bin == 0, pltpu.roll(previous, 128 - 4, 1), 0.0)
        load = pltpu.roll(whole, 128 - 20, 1)
        valid = (lane_full < 20) & (column_bin == family) & (row_bin < 4)
        return jnp.where(valid, load / jnp.where(valid, whole, 1.0), 0.0), valid

    to_column[1].wait_recv()
    to_column[gy - 1].wait_recv()
    wrap = lambda i: lax.rem(i + gy, gy)
    around = [across_gx(rows_of(wrap(n + d))) for d in (-1, 0, 1)]
    rate_here, _ = rates_of(around[1], around[0])
    rate_next, _ = rates_of(around[2], around[1])

    def pick(table, dm, lane):
        hit = (row_full == lax.rem(m + dm + gx, gx)) & (lane_full == lane)
        value = jnp.sum(jnp.where(hit, table, 0.0), axis=0, keepdims=True)
        return jnp.sum(value, axis=1, keepdims=True)

    local = []
    for f in range(2):
        for b in range(NBINS):
            col, row = b // 5, b % 5
            table = rate_here if row < 4 else rate_next
            local.append(pick(table, col - f, 15 * f + row % 4))

    outs = []
    for xb in range(CX // 8):
        bins = bins_of(xb)
        rated = []
        for f in range(2):
            value = jnp.zeros((8, 128), f32)
            for b in range(NBINS):
                value = jnp.where(bins[f] == b, local[10 * f + b], value)
            rated.append(value)
        own = slice(8 * xb, 8 * xb + 8)
        for g in range(4):
            turned = [roll(value, 32 * g) for value in rated]
            for z in range(4 * g, 4 * g + 4):
                for axis in range(3):
                    mix = turned[0] * flux[0, axis, z, own, :] + turned[1] * flux[1, axis, z, own, :]
                    staged[axis, z, own, :] = roll(mix, -32 * g)
        copy = pltpu.make_async_copy(staged.at[:, :, own], fine.at[:, :, own], out_sem.at[xb])
        copy.start()
        outs.append(copy)

    for d in order[2:]:
        to_column[d].wait_recv()
    crossed = [across_gx(rows_of(i)) for i in range(gy)]
    found = [jnp.zeros((gx, 128), f32) for _ in range(8)]
    half = (columns // 2) << row_bits
    for i in range(gy):
        rate, valid = rates_of(crossed[i], crossed[i - 1])
        pair = family * half + (row_full << row_bits) + 4 * i + row_bin
        pair = jnp.where(valid, pair, -1)
        for j in range(8):
            found[j] += jnp.where(pair == owned[j], rate, 0.0)
    line = jnp.zeros((1, 128), f32)
    for j in range(8):
        value = jnp.sum(jnp.sum(found[j], axis=0, keepdims=True), axis=1, keepdims=True)
        line += jnp.where(lane_row == j, value, 0.0)
    coarse[...] = line[:, :8]

    for d in order:
        to_column[d].wait_send()
    for copy in outs:
        copy.wait()


def solution(mesh):
    gx, gy = mesh.shape["gx"], mesh.shape["gy"]

    def shards(conductivity, well_rates, block_label, owned_pairs):
        vmem, dma = pltpu.VMEM, pltpu.SemaphoreType.DMA
        any_space = pl.BlockSpec(memory_space=pl.ANY)
        fine, coarse = pl.pallas_call(
            functools.partial(kernel, gx, gy),
            name="basis_flux",
            out_shape=(
                jax.ShapeDtypeStruct((3, NZ, CX, CY), f32),
                jax.ShapeDtypeStruct((1, 8), f32),
            ),
            in_specs=[any_space, any_space, any_space, pl.BlockSpec(memory_space=pltpu.SMEM)],
            out_specs=(any_space, pl.BlockSpec(memory_space=pltpu.VMEM)),
            scratch_shapes=[
                vmem((NZ, EXT, CY), f32),
                vmem((EXT, CY), jnp.int32),
                vmem((NZ, CX, CY), f32),
                vmem((3, CX, CY), f32),
                vmem((3, CX, CY), f32),
                vmem((3, EXT, CY), f32),
                vmem((3, EXT, CY), f32),
                vmem((20, ROWS, 128), f32),
                vmem((2, 5, ROWS, 128), jnp.int32),
                vmem((2, 20, ROWS, 128), f32),
                vmem((2, 20, ROWS, 128), f32),
                vmem((2, 20, ROWS, 128), f32),
                vmem((20, ROWS, 128), f32),
                vmem((5, ROWS, 128), f32),
                vmem((2, 20, ROWS, 128), f32),
                vmem((2, 5, ROWS, 128), f32),
                vmem((2, 2, 20, ROWS, 128), f32),
                vmem((2, 3, NZ, CX, CY), f32),
                vmem((2, 2, CX, CY), f32),
                vmem((1, 1, 128), f32),
                vmem((gx * gy, 1, 128), f32),
                vmem((3, NZ, CX, CY), f32),
                dma((3,)),
                dma((CX // 8,)),
                dma((10,)),
                dma((10,)),
                dma((gx,)),
                dma((gx,)),
                dma((gy,)),
                dma((gy,)),
            ],
            compiler_params=pltpu.CompilerParams(
                collective_id=0, has_side_effects=True, vmem_limit_bytes=60 * 1024 * 1024
            ),
        )(conductivity, well_rates, block_label, owned_pairs)
        return fine, coarse.reshape(8)

    in_specs = (P(None, "gx", "gy"), P(None, "gx", "gy"), P("gx", "gy"), P(("gx", "gy")))
    out_specs = (P(None, None, "gx", "gy"), P(("gx", "gy")))
    return jax.shard_map(shards, mesh=mesh, in_specs=in_specs, out_specs=out_specs, check_vma=False)
```

time: 624 us -> 72.4 us (0.12)
  other arithmetic: 400 us -> 0 us
  local copies, waits for them, and re-layouts: 173 us -> 3.24 us
  Pallas kernels: 0 us -> 68.4 us
  blocking collectives: 26.7 us -> 0 us
  waiting for transfers between devices: 11.9 us -> 0 us
  starting transfers between devices: 8.02 us -> 0 us
    scatter-add x2 -> x0, other arithmetic: 227 us -> none  [the longest x1 113 us: shards(): jax.ops.segment_sum(energy.reshape(-1), flat_ids, num_segments=pair_count)]
    add x13 -> x0, other arithmetic: 147 us -> none  [the longest x12 147 us: sweep(): return centre + RELAXATION * (source_full - applied) / diag_full]
    slice x30 -> x0, local copies, waits for them, and re-layouts: 78 us -> none  [the longest x13 44.8 us: shift_up(): return jnp.concatenate([field[:, 1:], jnp.zeros_like(field[:, :1])], axis=1)]
    pallas_call x0 -> x1, Pallas kernels: none -> 68.4 us  [shards(): pl.pallas_call(functools.partial(kernel, gx, gy), name='basis_flux', out_...]
    gather x2 -> x0, local copies, waits for them, and re-layouts: 65.9 us -> none  [the longest x1 65.3 us: shards(): weight = jnp.take(all_rates, ids_own)[:, None]]
    while x36 -> x0, local copies, waits for them, and re-layouts: 28.6 us -> none
    psum x4 -> x0, blocking collectives: 26.7 us -> none  [by_axis(): x = lax.psum(x, axis)]
    ppermute x4 -> x0, waiting for transfers between devices: 11.9 us -> none  [the longest x2 9.4 us: with_halo(): lax.ppermute(lax.slice_in_dim(block, block.shape[dim] - width, None, axis...]
  transfers between devices with their start and end apart: 4 -> 0, of which waited for: 3 -> 0; matrix products, arithmetic and copies ran while one was open for 0% -> 0% of each run, Pallas kernels for 0% -> 0%
where the time goes in v1:
time: 72.4 us; the launch traced here: 72.3 us
  Pallas kernels  68.4 us (94%)
  local copies, waits for them, and re-layouts  3.24 us (4%)
    pallas_call x1, Pallas kernels, shards(): pl.pallas_call(functools.partial(kernel, gx, gy), name='basis_flux', out_...  68.4 us
    unnamed x4, local copies, waits for them, and re-layouts  3.24 us

profile of v1, /device:TPU:1, one launch (start us, length us, event | category | flops | bytes accessed | tf_op | source)
XLA Modules:
  0.0 72.3 jit_solution(371497444745834031)
XLA Ops:
  0.6 68.4 %basis_flux.1 = (f32[3,16,64,128]{3,2,1,0:T(8,128)}, f32[1,8]{1,0:T(1,128)}) custom-call(f32[16,64,128]{2,1,0:T(8,128)} %cond.1, f32[16,64,128]{2,1,0:T(8,128)} %well.1, s32[64,128]{1,0:T(8,128)} %label.1, s32[8]{0:T(128)} %owned.1), custom_call_target="tpu_custom_call" | custom-call | tf_op jit(solution)/shard_map/basis_flux/pallas_call | solution.py:467
  69.0 0.0 copy-start
  69.0 2.7 %copy.8 = f32[3,16,64,128]{3,2,1,0:T(8,128)} copy(f32[3,16,64,128]{3,2,1,0:T(8,128)} %get-tuple-element.8) | data formatting | bytes 3145728
  71.7 0.0 copy-done
  71.7 0.5 copy.9
Async XLA Ops:
  69.0 2.7 %copy-start = (f32[1,8]{1,0:T(1,128)S(1)}, f32[1,8]{1,0:T(1,128)}, u32[]{:S(2)}) copy-start(f32[1,8]{1,0:T(1,128)} %get-tuple-element.5) | copy-start | bytes 100

commit v2 on v1

v2 whole, which is shorter than its diff:
```python
import functools

import jax
import jax.numpy as jnp
from jax import lax
from jax.experimental import pallas as pl
from jax.experimental.pallas import tpu as pltpu
from jax.sharding import PartitionSpec as P

ITERS = 13
REACTION = 0.05
RELAXATION = 0.8
NZ = 16
CX = 64
CY = 128
HALO = 16
EXT = CX + 2 * HALO
PAD = 8
ROWS = EXT + 2 * PAD
PHASES = 5
NV = 4 * PHASES
NBINS = 10
MESH = pl.DeviceIdType.MESH
f32 = jnp.float32


def lane_iota():
    return lax.broadcasted_iota(jnp.int32, (8, 128), 1)


def roll(value, shift):
    return pltpu.roll(value, shift % 128, 1)


def take(value, lanes):
    return jnp.take_along_axis(value, lanes, axis=1, mode="promise_in_bounds")


def rows8(start):
    return pl.ds(pl.multiple_of(start, 8), 8)


def right_of(v, i):
    k, f = divmod(i, PHASES)
    return v[i + 1] if f < PHASES - 1 else roll(v[PHASES * k], -1)


def left_of(v, i):
    k, f = divmod(i, PHASES)
    return v[i - 1] if f > 0 else roll(v[PHASES * k + PHASES - 1], 1)


def above_of(v, i):
    k, f = divmod(i, PHASES)
    return v[i + PHASES] if k < 3 else roll(v[f], -32)


def below_of(v, i):
    k, f = divmod(i, PHASES)
    return v[i - PHASES] if k > 0 else roll(v[3 * PHASES + f], 32)


class Lanes:
    def __init__(self, residue=None):
        lane = lane_iota()
        self.lane = lane
        self.group = lane >> 5
        self.inner = lane & 31
        if residue is None:
            residue = [((lane - 2 * g) & 127) % PHASES for g in range(4)]
        self.residue = residue

    def column(self, f):
        return PHASES * self.inner + f

    def outside(self, f):
        y = self.column(f)
        return (y < HALO) | (y >= HALO + CY)

    def main(self, f):
        return (self.column(f) - HALO + 2 * self.group) & 127

    def plain(self, f):
        return (self.column(f) - HALO) & 127

    def strip(self, f):
        y = self.column(f)
        return (32 * self.group + jnp.where(y < HALO, y - HALO, y - HALO - CY)) & 127

    def back(self, f):
        found = jnp.zeros_like(self.lane)
        for g in range(4):
            y = (self.lane - 2 * g) & 127
            j = (y + HALO - f) // PHASES
            found = jnp.where(self.residue[g] == (f + 4) % PHASES, 32 * g + j, found)
        return found

    def spread(self, natural, tables):
        out = []
        for k in range(4):
            turned = [roll(natural[4 * g + k], 2 * g) if g else natural[k] for g in range(4)]
            for f in range(PHASES):
                merged = turned[0]
                for g in range(1, 4):
                    merged = jnp.where(self.residue[g] == (f + 4) % PHASES, turned[g], merged)
                out.append(take(merged, tables[f]))
        return out

    def gather_back(self, phases, tables):
        out = [None] * NZ
        for k in range(4):
            moved = [take(phases[PHASES * k + f], tables[f]) for f in range(PHASES)]
            for g in range(4):
                merged = moved[0]
                for f in range(1, PHASES):
                    merged = jnp.where(self.residue[g] == (f + 4) % PHASES, moved[f], merged)
                out[4 * g + k] = roll(merged, -2 * g) if g else merged
        return out

    def compose(self, own):
        around = ((self.lane + 16) & 127) >> 5
        low = jnp.where(around < 1, own[0], own[1])
        return jnp.where(around < 2, low, jnp.where(around < 3, own[2], own[3]))

    def squeeze(self, v):
        even, low = (self.group & 1) == 0, self.group < 2
        return jnp.where(low, jnp.where(even, v[0], v[1]), jnp.where(even, v[2], v[3]))

    def fold(self, v):
        even, low = (self.group & 1) == 0, self.group < 2
        halves = []
        for a, b in ((v[0], v[1]), (v[2], v[3])):
            halves.append(jnp.where(even, a, b) + roll(jnp.where(even, b, a), -32))
        four = jnp.where(low, halves[0], halves[1]) + roll(jnp.where(low, halves[1], halves[0]), -64)
        last = v[4] + roll(v[4], 32)
        return four, last + roll(last, 64)


def harmonic(one, other):
    return 2.0 * one * other / (one + other)


def pair_ids(label, row_bits, columns):
    column = label >> row_bits
    row = label & ((1 << row_bits) - 1)
    first = ((column >> 1) << row_bits) + row
    second = ((((column + columns - 1) & (columns - 1)) >> 1) << row_bits) + row + ((columns // 2) << row_bits)
    sign = jnp.where((column & 1) == 0, 1.0, -1.0).astype(f32)
    return first, second, sign


def kernel(gx, gy, cond, well, label, owned, fine, coarse, ce, le, wl, send_l, send_r, from_l, from_r, tables,
           c, tags, ids, tx, ty, tyb, hz, w, signs, s, p, wells, flux, sums, natural, part, gathered,
           local_sem, halo_send, halo_recv, row_send, row_recv, col_send, col_recv):
    m, n = lax.axis_index("gx"), lax.axis_index("gy")
    row_bits = (4 * gy).bit_length() - 1
    columns = 2 * gx

    def at(dm, dn):
        return (lax.rem(m + dm + gx, gx), lax.rem(n + dn + gy, gy))

    partners = [at(d, 0) for d in range(1, gx)] + [at(0, d) for d in range(1, gy)]
    partners += [at(a, b) for a in (-1, 1) for b in (-1, 1)]
    barrier = pltpu.get_barrier_semaphore()
    for partner in partners:
        pl.semaphore_signal(barrier, inc=1, device_id=partner, device_id_type=MESH)

    own_rows = pl.ds(HALO, CX)
    loads = [
        pltpu.make_async_copy(cond, ce.at[:, own_rows], local_sem.at[0]),
        pltpu.make_async_copy(label, le.at[own_rows], local_sem.at[1]),
        pltpu.make_async_copy(well, wl, local_sem.at[2]),
    ]
    for load in loads:
        load.start()

    for f in range(2):
        tx[f, :, :PAD, :] = jnp.zeros((NV, PAD, 128), f32)
        for slot in range(2):
            p[slot, f, :, :PAD, :] = jnp.zeros((NV, PAD, 128), f32)
            p[slot, f, :, ROWS - PAD :, :] = jnp.zeros((NV, PAD, 128), f32)
        ids[f, :, ROWS - PAD :, :] = jnp.zeros((PHASES, PAD, 128), jnp.int32)
    c[:, ROWS - PAD :, :] = jnp.ones((NV, PAD, 128), f32)
    lanes = Lanes()
    for f in range(PHASES):
        tables[0, f] = lanes.main(f)
        tables[1, f] = lanes.strip(f)
        tables[2, f] = lanes.plain(f)
        tables[3, f] = lanes.back(f)
    for g in range(4):
        tables[4, g] = lanes.residue[g]

    loads[0].wait()
    loads[1].wait()

    def pack(xb, carry):
        lanes = Lanes()
        rows, out = rows8(HALO + 8 * xb), rows8(8 * xb)
        right_half = lanes.inner < 16
        mixed = [
            lanes.compose([roll(ce[4 * g + k, rows, :], 32 * g) for g in range(4)]) for k in range(4)
        ]
        for h in range(2):
            even, odd = mixed[2 * h], roll(mixed[2 * h + 1], 16)
            send_l[h, out, :] = jnp.where(right_half, even, odd)
            send_r[h, out, :] = jnp.where(right_half, odd, even)
        own = le[rows, :].astype(f32)
        marks = lanes.compose([roll(own, 32 * g) for g in range(4)])
        send_l[2, out, :] = marks
        send_r[2, out, :] = marks
        return carry

    lax.fori_loop(0, CX // 8, pack, 0)
    pl.semaphore_wait(barrier, len(partners))

    low, high = pl.ds(0, HALO), pl.ds(CX - HALO, HALO)
    below, above = pl.ds(0, HALO), pl.ds(HALO + CX, HALO)
    moves = [
        (cond.at[:, low], ce.at[:, above], at(-1, 0)),
        (cond.at[:, high], ce.at[:, below], at(1, 0)),
        (label.at[low], le.at[above], at(-1, 0)),
        (label.at[high], le.at[below], at(1, 0)),
        (send_l, from_r.at[:, own_rows], at(0, -1)),
        (send_r, from_l.at[:, own_rows], at(0, 1)),
        (send_l.at[:, low], from_r.at[:, above], at(-1, -1)),
        (send_l.at[:, high], from_r.at[:, below], at(1, -1)),
        (send_r.at[:, low], from_l.at[:, above], at(-1, 1)),
        (send_r.at[:, high], from_l.at[:, below], at(1, 1)),
    ]
    halos = [
        pltpu.make_async_remote_copy(src, dst, halo_send.at[i], halo_recv.at[i], device_id=to, device_id_type=MESH)
        for i, (src, dst, to) in enumerate(moves)
    ]
    for halo in halos:
        halo.start()

    def spread_own(xb, carry):
        lanes = Lanes([tables[4, g] for g in range(4)])
        rows, out = rows8(8 * xb), rows8(PAD + 8 * xb)
        main = [tables[0, f] for f in range(PHASES)]
        for i, value in enumerate(lanes.spread([ce[z, rows, :] for z in range(NZ)], main)):
            c[i, out, :] = value
        own = le[rows, :].astype(f32)
        for f in range(PHASES):
            tags[f, out, :] = take(own, tables[2, f])
        return carry

    def spread_wells(xb, carry):
        lanes = Lanes([tables[4, g] for g in range(4)])
        rows = rows8(8 * xb)
        main = [tables[0, f] for f in range(PHASES)]
        for i, value in enumerate(lanes.spread([wl[z, rows, :] for z in range(NZ)], main)):
            wells[i, rows, :] = value
        return carry

    lax.fori_loop(HALO // 8, (HALO + CX) // 8, spread_own, 0)
    loads[2].wait()
    lax.fori_loop(0, CX // 8, spread_wells, 0)
    for halo in halos:
        halo.wait()
    lax.fori_loop(0, HALO // 8, spread_own, 0)
    lax.fori_loop((HALO + CX) // 8, EXT // 8, spread_own, 0)

    def add_strips(xb, carry):
        lanes = Lanes()
        rows, out = rows8(8 * xb), rows8(PAD + 8 * xb)
        right_half = lanes.inner < 16
        strips = []
        for h in range(2):
            right, left = from_r[h, rows, :], from_l[h, rows, :]
            strips.append(jnp.where(right_half, right, left))
            strips.append(roll(jnp.where(right_half, left, right), -16))
        marks = jnp.where(right_half, from_r[2, rows, :], from_l[2, rows, :])
        for f in range(PHASES):
            outside, table = lanes.outside(f), tables[1, f]
            for k in range(4):
                i = PHASES * k + f
                c[i, out, :] = jnp.where(outside, take(strips[k], table), c[i, out, :])
            tag = jnp.where(outside, take(marks, table), tags[f, out, :]).astype(jnp.int32)
            first, second, sign = pair_ids(tag, row_bits, columns)
            ids[0, f, out, :] = first
            ids[1, f, out, :] = second
            s[f, out, :] = sign
        return carry

    lax.fori_loop(0, EXT // 8, add_strips, 0)

    def faces(xb, carry):
        group = lane_iota() >> 5
        a = PAD + 8 * xb
        here, ahead = rows8(a), pl.ds(a + 1, 8)
        cs = [c[i, here, :] for i in range(NV)]
        hx = [harmonic(cs[i], c[i, ahead, :]) for i in range(NV)]
        hy = [harmonic(cs[i], right_of(cs, i)) for i in range(NV)]
        for i in range(NV):
            face = harmonic(cs[i], above_of(cs, i))
            if i >= 3 * PHASES:
                face = jnp.where(group == 3, 0.0, face)
                hz[i - 3 * PHASES, here, :] = roll(face, 32)
            hz[PHASES + i, here, :] = face
        for f in range(2):
            pid = [ids[f, phase, here, :] for phase in range(PHASES)]
            same_x = [pid[phase] == ids[f, phase, ahead, :] for phase in range(PHASES)]
            same_y = [pid[phase] == right_of(pid, phase) for phase in range(PHASES)]
            tys = [jnp.where(same_y[i % PHASES], hy[i], 0.0) for i in range(NV)]
            for i in range(NV):
                tx[f, i, here, :] = jnp.where(same_x[i % PHASES], hx[i], 0.0)
                ty[f, i, here, :] = tys[i]
                if i % PHASES == 0:
                    tyb[f, i // PHASES, here, :] = left_of(tys, i)
        return carry

    lax.fori_loop(0, EXT // 8, faces, 0)

    def weights(it, carry):
        f, xb = it & 1, it >> 1
        a = PAD + 8 * xb
        here, behind = rows8(a), pl.ds(a - 1, 8)
        turn = jnp.where(f == 0, 1.0, -1.0).astype(f32)
        for phase in range(PHASES):
            source = turn * s[phase, here, :]
            signs[f, phase, here, :] = source
            for k in range(4):
                i = PHASES * k + phase
                left = tyb[f, k, here, :] if phase == 0 else ty[f, i - 1, here, :]
                total = REACTION + tx[f, i, here, :] + tx[f, i, behind, :] + ty[f, i, here, :] + left
                total += hz[PHASES + i, here, :] + hz[i, here, :]
                scale = RELAXATION / total
                w[f, i, here, :] = scale
                p[0, f, i, here, :] = source * scale
        return carry

    lax.fori_loop(0, 2 * (EXT // 8), weights, 0)

    def relax(src, f, a, ups):
        here, ahead, behind = pl.ds(a, 8), pl.ds(a + 1, 8), pl.ds(a - 1, 8)
        ps = [p[src, f, i, here, :] for i in range(NV)]
        tys = [ty[f, i, here, :] for i in range(NV)]
        for i in range(NV):
            k, phase = divmod(i, PHASES)
            total = signs[f, phase, here, :] + tx[f, i, here, :] * p[src, f, i, ahead, :]
            total += tx[f, i, behind, :] * p[src, f, i, behind, :]
            total += tys[i] * right_of(ps, i)
            total += (tys[i - 1] if phase > 0 else tyb[f, k, here, :]) * left_of(ps, i)
            total += ups[PHASES + i] * above_of(ps, i)
            total += ups[i] * below_of(ps, i)
            p[1 - src, f, i, here, :] = (1.0 - RELAXATION) * ps[i] + w[f, i, here, :] * total

    def sweep(src, first, last):
        def step(xb, carry):
            a = PAD + first + 8 * xb
            ups = [hz[i, pl.ds(a, 8), :] for i in range(NV + PHASES)]
            relax(src, 0, a, ups)
            relax(src, 1, a, ups)
            return carry

        lax.fori_loop(0, -(-(last - first) // 8), step, 0)

    for k in range(2, ITERS + 1):
        first = HALO - (ITERS - k)
        last = HALO + CX + (ITERS - k) + 1
        sweep(k % 2, first, last)
    done = (ITERS + 1) % 2

    def fluxes(it, carry):
        f, xb = it & 1, it >> 1
        lanes = Lanes()
        a = PAD + HALO + 8 * xb
        here, ahead, own = rows8(a), pl.ds(a + 1, 8), rows8(8 * xb)
        ps = [p[done, f, i, here, :] for i in range(NV)]
        energy, load = [None] * PHASES, [None] * PHASES
        for i in range(NV):
            phase = i % PHASES
            dx = ps[i] - p[done, f, i, ahead, :]
            dy = ps[i] - right_of(ps, i)
            dz = ps[i] - above_of(ps, i)
            vx = tx[f, i, here, :] * dx
            vy = ty[f, i, here, :] * dy
            vz = hz[PHASES + i, here, :] * dz
            flux[f, 0, i, own, :] = vx
            flux[f, 1, i, own, :] = vy
            flux[f, 2, i, own, :] = vz
            cell = vx * dx + vy * dy + vz * dz + REACTION * ps[i] * ps[i]
            rated = wells[i, own, :] * ps[i]
            energy[phase] = cell if i < PHASES else energy[phase] + cell
            load[phase] = rated if i < PHASES else load[phase] + rated
        for q, value in enumerate((energy, load)):
            four, last = lanes.fold(value)
            sums[f, q, 0, own, :] = four
            sums[f, q, 1, own, :] = last
        return carry

    lax.fori_loop(0, 2 * (CX // 8), fluxes, 0)

    def bins_of(marks):
        column = ((marks >> row_bits) - 2 * m) & (columns - 1)
        row = ((marks & ((1 << row_bits) - 1)) - 4 * n) & ((1 << row_bits) - 1)
        return [jnp.where(column >= edge, 5, 0) + row for edge in (2, 1)]

    lanes = Lanes()
    inside = [lanes.squeeze([jnp.where(lanes.outside(f), 0, 1) for f in range(4)]),
              jnp.where(lanes.outside(4) | (lanes.group > 0), 0, 1)]
    totals = [[[jnp.zeros((8, 128), f32) for _ in range(NBINS)] for _ in range(2)] for _ in range(2)]
    for xb in range(CX // 8):
        at_rows = slice(PAD + HALO + 8 * xb, PAD + HALO + 8 * xb + 8)
        marks = [tags[f, at_rows, :] for f in range(PHASES)]
        for half, mark in enumerate((lanes.squeeze(marks), marks[4])):
            bins = bins_of(mark.astype(jnp.int32))
            for f in range(2):
                index = jnp.where(inside[half] == 1, bins[f], -1)
                cells = [sums[f, q, half, 8 * xb : 8 * xb + 8, :] for q in range(2)]
                for b in range(NBINS):
                    hit = index == b
                    for q in range(2):
                        totals[q][f][b] += jnp.where(hit, cells[q], 0.0)
    lines = jnp.zeros((8, 128), f32)
    for q in range(2):
        for f in range(2):
            for b in range(NBINS):
                value = jnp.sum(totals[q][f][b], axis=1, keepdims=True)
                lines = jnp.where(lanes.lane == 20 * q + 10 * f + b, value, lines)
    line = jnp.sum(lines, axis=0, keepdims=True)
    part[0] = line
    mine = n * gx + m
    gathered[pl.ds(mine, 1)] = line[None]

    to_row = [
        pltpu.make_async_remote_copy(
            part, gathered.at[pl.ds(mine, 1)], row_send.at[d], row_recv.at[d], device_id=at(d, 0), device_id_type=MESH
        )
        for d in range(1, gx)
    ]
    for copy in to_row:
        copy.start()

    def return_fluxes(it, carry):
        lanes = Lanes([tables[4, g] for g in range(4)])
        own, t = rows8(8 * (it // 3)), it % 3
        back = [tables[3, phase] for phase in range(PHASES)]
        for f in range(2):
            out = lanes.gather_back([flux[f, t, i, own, :] for i in range(NV)], back)
            for z in range(NZ):
                natural[f, t, z, own, :] = out[z]
        return carry

    steps = 3 * (CX // 8)
    lax.fori_loop(0, steps // 2, return_fluxes, 0)
    for copy in to_row:
        copy.wait()
    block = pl.ds(n * gx, gx)
    order = sorted(range(1, gy), key=lambda d: min(d, gy - d))
    to_column = {
        d: pltpu.make_async_remote_copy(
            gathered.at[block], gathered.at[block], col_send.at[d], col_recv.at[d], device_id=at(0, d), device_id_type=MESH
        )
        for d in order
    }
    for d in order:
        to_column[d].start()
    lax.fori_loop(steps // 2, steps, return_fluxes, 0)

    lane_full = lax.broadcasted_iota(jnp.int32, (gx, 128), 1)
    row_full = lax.broadcasted_iota(jnp.int32, (gx, 128), 0)
    entry = lane_full % 20
    family = entry // 10
    column_bin = (entry // 5) & 1
    row_bin = entry % 5

    def rows_of(at_n):
        return jnp.concatenate([gathered[at_n * gx + i] for i in range(gx)], axis=0)

    def across_gx(value):
        before = pltpu.roll(pltpu.roll(value, 1, 0), 128 - 5, 1)
        after = pltpu.roll(pltpu.roll(value, gx - 1, 0), 5, 1)
        return value + jnp.where(family == 0, before, after)

    def rates_of(value, previous):
        whole = value + jnp.where(row_bin == 0, pltpu.roll(previous, 128 - 4, 1), 0.0)
        load = pltpu.roll(whole, 128 - 20, 1)
        valid = (lane_full < 20) & (column_bin == family) & (row_bin < 4)
        return jnp.where(valid, load / jnp.where(valid, whole, 1.0), 0.0), valid

    to_column[1].wait_recv()
    to_column[gy - 1].wait_recv()
    around = [across_gx(rows_of(lax.rem(n + d + gy, gy))) for d in (-1, 0, 1)]
    near = [rates_of(around[1], around[0])[0], rates_of(around[2], around[1])[0]]

    def pick_row(table, dm):
        hit = row_full == lax.rem(m + dm + gx, gx)
        return jnp.sum(jnp.where(hit, table, 0.0), axis=0, keepdims=True)

    picked = {(t, dm): pick_row(near[t], dm) for t in range(2) for dm in (-1, 0, 1)}
    local = []
    for f in range(2):
        for b in range(NBINS):
            col, row = b // 5, b % 5
            lane = 15 * f + row % 4
            local.append(picked[row // 4, col - f][:, lane : lane + 1])

    def mix(xb, carry):
        own = rows8(8 * xb)
        bins = bins_of(le[rows8(HALO + 8 * xb), :])
        rated = []
        for f in range(2):
            value = jnp.zeros((8, 128), f32)
            for b in range(NBINS):
                value = jnp.where(bins[f] == b, local[10 * f + b], value)
            rated.append(value)
        for z in range(NZ):
            for axis in range(3):
                fine[axis, z, own, :] = rated[0] * natural[0, axis, z, own, :] + rated[1] * natural[1, axis, z, own, :]
        return carry

    lax.fori_loop(0, CX // 8, mix, 0)

    for d in order[2:]:
        to_column[d].wait_recv()
    crossed = [across_gx(rows_of(i)) for i in range(gy)]
    found = [jnp.zeros((gx, 128), f32) for _ in range(8)]
    half = (columns // 2) << row_bits
    for i in range(gy):
        rate, valid = rates_of(crossed[i], crossed[i - 1])
        pair = family * half + (row_full << row_bits) + 4 * i + row_bin
        pair = jnp.where(valid, pair, -1)
        for j in range(8):
            found[j] += jnp.where(pair == owned[j], rate, 0.0)
    lines = jnp.zeros((gx, 128), f32)
    for j in range(8):
        value = jnp.sum(found[j], axis=1, keepdims=True)
        lines = jnp.where(lane_full == j, value, lines)
    coarse[...] = jnp.sum(lines, axis=0, keepdims=True)[:, :8]

    for d in order:
        to_column[d].wait_send()


def solution(mesh):
    gx, gy = mesh.shape["gx"], mesh.shape["gy"]

    def shards(conductivity, well_rates, block_label, owned_pairs):
        vmem, dma = pltpu.VMEM, pltpu.SemaphoreType.DMA
        any_space = pl.BlockSpec(memory_space=pl.ANY)
        fine, coarse = pl.pallas_call(
            functools.partial(kernel, gx, gy),
            name="basis_flux",
            out_shape=(
                pltpu.VMEM((3, NZ, CX, CY), f32),
                jax.ShapeDtypeStruct((1, 8), f32),
            ),
            in_specs=[any_space, any_space, any_space, pl.BlockSpec(memory_space=pltpu.SMEM)],
            out_specs=(pl.BlockSpec(memory_space=pltpu.VMEM), pl.BlockSpec(memory_space=pltpu.VMEM)),
            scratch_shapes=[
                vmem((NZ, EXT, CY), f32),
                vmem((EXT, CY), jnp.int32),
                vmem((NZ, CX, CY), f32),
                vmem((3, CX, CY), f32),
                vmem((3, CX, CY), f32),
                vmem((3, EXT, CY), f32),
                vmem((3, EXT, CY), f32),
                vmem((5, PHASES, 8, 128), jnp.int32),
                vmem((NV, ROWS, 128), f32),
                vmem((PHASES, ROWS, 128), f32),
                vmem((2, PHASES, ROWS, 128), jnp.int32),
                vmem((2, NV, ROWS, 128), f32),
                vmem((2, NV, ROWS, 128), f32),
                vmem((2, 4, ROWS, 128), f32),
                vmem((NV + PHASES, ROWS, 128), f32),
                vmem((2, NV, ROWS, 128), f32),
                vmem((2, PHASES, ROWS, 128), f32),
                vmem((PHASES, ROWS, 128), f32),
                vmem((2, 2, NV, ROWS, 128), f32),
                vmem((NV, CX, 128), f32),
                vmem((2, 3, NV, CX, 128), f32),
                vmem((2, 2, 2, CX, 128), f32),
                vmem((2, 3, NZ, CX, CY), f32),
                vmem((1, 1, 128), f32),
                vmem((gx * gy, 1, 128), f32),
                dma((3,)),
                dma((10,)),
                dma((10,)),
                dma((gx,)),
                dma((gx,)),
                dma((gy,)),
                dma((gy,)),
            ],
            compiler_params=pltpu.CompilerParams(
                collective_id=0, has_side_effects=True, vmem_limit_bytes=65_400_000
            ),
        )(conductivity, well_rates, block_label, owned_pairs)
        return fine, coarse.reshape(8)

    in_specs = (P(None, "gx", "gy"), P(None, "gx", "gy"), P("gx", "gy"), P(("gx", "gy")))
    out_specs = (P(None, None, "gx", "gy"), P(("gx", "gy")))
    return jax.shard_map(shards, mesh=mesh, in_specs=in_specs, out_specs=out_specs, check_vma=False)
```

time: 72.4 us -> 57.6 us (0.80)
  Pallas kernels: 68.4 us -> 55.1 us
  local copies, waits for them, and re-layouts: 3.24 us -> 1.66 us
    pallas_call x1, Pallas kernels: 68.4 us -> 55.1 us  [shards(): pl.pallas_call(functools.partial(kernel, gx, gy), name='basis_flux', out_...]
    unnamed x4, local copies, waits for them, and re-layouts: 3.24 us -> 1.66 us
where the time goes in v2:
time: 57.6 us; the launch traced here: 57.4 us
  Pallas kernels  55.1 us (96%)
  local copies, waits for them, and re-layouts  1.66 us (3%)
  between operations  0.65 us (1%)
    pallas_call x1, Pallas kernels, shards(): pl.pallas_call(functools.partial(kernel, gx, gy), name='basis_flux', out_...  55.1 us
    unnamed x4, local copies, waits for them, and re-layouts  1.66 us

profile of v2, /device:TPU:1, one launch (start us, length us, event | category | flops | bytes accessed | tf_op | source)
XLA Modules:
  0.0 57.4 jit_solution(15313926376448371099)
XLA Ops:
  0.6 55.1 %basis_flux.1 = (f32[3,16,64,128]{3,2,1,0:T(8,128)S(1)}, f32[1,8]{1,0:T(1,128)}) custom-call(f32[16,64,128]{2,1,0:T(8,128)} %cond.1, f32[16,64,128]{2,1,0:T(8,128)} %well.1, s32[64,128]{1,0:T(8,128)} %label.1, s32[8]{0:T(128)} %owned.1), custom_call_target="tpu_custom_call" | custom-call | tf_op jit(solution)/shard_map/basis_flux/pallas_call | solution.py:543
  55.8 0.0 copy-start
  55.8 1.1 %copy.8 = f32[3,16,64,128]{3,2,1,0:T(8,128)} copy(f32[3,16,64,128]{3,2,1,0:T(8,128)S(1)} %get-tuple-element.6) | data formatting | bytes 3145728
  56.9 0.0 copy-done
  56.9 0.5 copy.9
Async XLA Ops:
  55.8 1.2 %copy-start = (f32[1,8]{1,0:T(1,128)S(1)}, f32[1,8]{1,0:T(1,128)}, u32[]{:S(2)}) copy-start(f32[1,8]{1,0:T(1,128)} %get-tuple-element.5) | copy-start | bytes 100

commit v3 on v2

--- a/solution.py
+++ b/solution.py
@@ -60,6 +60,15 @@
     return v[i - PHASES] if k > 0 else roll(v[3 * PHASES + f], 32)
 
 
+def each(low, high, body, step):
+    def group(i, carry):
+        for j in range(step):
+            body(low + step * i + j, carry)
+        return carry
+
+    lax.fori_loop(0, (high - low) // step, group, 0)
+
+
 class Lanes:
     def __init__(self, residue=None):
         lane = lane_iota()
@@ -210,7 +219,7 @@
         send_r[2, out, :] = marks
         return carry
 
-    lax.fori_loop(0, CX // 8, pack, 0)
+    each(0, CX // 8, pack, 4)
     pl.semaphore_wait(barrier, len(partners))
 
     low, high = pl.ds(0, HALO), pl.ds(CX - HALO, HALO)
@@ -253,13 +262,15 @@
             wells[i, rows, :] = value
         return carry
 
-    lax.fori_loop(HALO // 8, (HALO + CX) // 8, spread_own, 0)
+    each(HALO // 8, (HALO + CX) // 8, spread_own, 4)
     loads[2].wait()
-    lax.fori_loop(0, CX // 8, spread_wells, 0)
-    for halo in halos:
+    each(0, CX // 8, spread_wells, 4)
+    for halo in halos[:4]:
         halo.wait()
-    lax.fori_loop(0, HALO // 8, spread_own, 0)
-    lax.fori_loop((HALO + CX) // 8, EXT // 8, spread_own, 0)
+    each(0, HALO // 8, spread_own, 2)
+    each((HALO + CX) // 8, EXT // 8, spread_own, 2)
+    for halo in halos[4:]:
+        halo.wait()
 
     def add_strips(xb, carry):
         lanes = Lanes()
@@ -283,7 +294,7 @@
             s[f, out, :] = sign
         return carry
 
-    lax.fori_loop(0, EXT // 8, add_strips, 0)
+    each(0, EXT // 8, add_strips, 4)
 
     def faces(xb, carry):
         group = lane_iota() >> 5
@@ -310,7 +321,7 @@
                     tyb[f, i // PHASES, here, :] = left_of(tys, i)
         return carry
 
-    lax.fori_loop(0, EXT // 8, faces, 0)
+    each(0, EXT // 8, faces, 2)
 
     def weights(it, carry):
         f, xb = it & 1, it >> 1
@@ -390,7 +401,7 @@
             sums[f, q, 1, own, :] = last
         return carry
 
-    lax.fori_loop(0, 2 * (CX // 8), fluxes, 0)
+    each(0, 2 * (CX // 8), fluxes, 4)
 
     def bins_of(marks):
         column = ((marks >> row_bits) - 2 * m) & (columns - 1)
@@ -444,7 +455,7 @@
         return carry
 
     steps = 3 * (CX // 8)
-    lax.fori_loop(0, steps // 2, return_fluxes, 0)
+    each(0, steps // 2, return_fluxes, 2)
     for copy in to_row:
         copy.wait()
     block = pl.ds(n * gx, gx)
@@ -457,7 +468,7 @@
     }
     for d in order:
         to_column[d].start()
-    lax.fori_loop(steps // 2, steps, return_fluxes, 0)
+    each(steps // 2, steps, return_fluxes, 2)
 
     lane_full = lax.broadcasted_iota(jnp.int32, (gx, 128), 1)
     row_full = lax.broadcasted_iota(jnp.int32, (gx, 128), 0)

time: 57.6 us -> 52.9 us (0.918)
  Pallas kernels: 55.1 us -> 50.4 us
    pallas_call x1, Pallas kernels: 55.1 us -> 50.4 us  [shards(): pl.pallas_call(functools.partial(kernel, gx, gy), name='basis_flux', out_...]
where the time goes in v3:
time: 52.9 us; the launch traced here: 52.7 us
  Pallas kernels  50.4 us (95%)
  local copies, waits for them, and re-layouts  1.66 us (3%)
  between operations  0.65 us (1%)
    pallas_call x1, Pallas kernels, shards(): pl.pallas_call(functools.partial(kernel, gx, gy), name='basis_flux', out_...  50.4 us
    unnamed x4, local copies, waits for them, and re-layouts  1.66 us

profile of v3, /device:TPU:1, one launch (start us, length us, event | category | flops | bytes accessed | tf_op | source)
XLA Modules:
  0.0 52.7 jit_solution(6100129727448212778)
XLA Ops:
  0.6 50.4 %basis_flux.1 = (f32[3,16,64,128]{3,2,1,0:T(8,128)S(1)}, f32[1,8]{1,0:T(1,128)}) custom-call(f32[16,64,128]{2,1,0:T(8,128)} %cond.1, f32[16,64,128]{2,1,0:T(8,128)} %well.1, s32[64,128]{1,0:T(8,128)} %label.1, s32[8]{0:T(128)} %owned.1), custom_call_target="tpu_custom_call" | custom-call | tf_op jit(solution)/shard_map/basis_flux/pallas_call | solution.py:554
  51.1 0.0 copy-start
  51.1 1.1 %copy.8 = f32[3,16,64,128]{3,2,1,0:T(8,128)} copy(f32[3,16,64,128]{3,2,1,0:T(8,128)S(1)} %get-tuple-element.6) | data formatting | bytes 3145728
  52.2 0.0 copy-done
  52.2 0.5 copy.9
Async XLA Ops:
  51.1 1.2 %copy-start = (f32[1,8]{1,0:T(1,128)S(1)}, f32[1,8]{1,0:T(1,128)}, u32[]{:S(2)}) copy-start(f32[1,8]{1,0:T(1,128)} %get-tuple-element.5) | copy-start | bytes 100
